TPU v7x, 128 devices: a whole 4x4x4 slice. The times are simulated.
128 devices in a mesh: tok: 4 (over y_hi, core), blk: 32 (over x, z, y_lo).
Axes of the slice: x: 4, y: 4 (y_hi: 2, y_lo: 2; y = y_hi * 2 + y_lo), z: 4, core: 2. Of those that a mesh axis runs over, the one named last changes fastest.
Arguments:
- tokens: bfloat16 [64, 128, 10240], P('blk', None, 'tok'), may hold values from -6 to 6
- cotangent: bfloat16 [64, 128, 10240], P('blk', None, 'tok'), may hold values from -6 to 6
- right_up: bfloat16 [64, 512, 128], P('blk'), may hold values from -0.5 to 0.5
- left_up: bfloat16 [512, 64, 64], P('blk'), may hold values from -0.75 to 0.75
- left_down: bfloat16 [512, 64, 64], P('blk'), may hold values from -0.75 to 0.75
- right_down: bfloat16 [64, 128, 512], P('blk'), may hold values from -0.25 to 0.25
Outputs:
- output: bfloat16 [64, 128, 10240], P('blk', None, 'tok')
- grad_tokens: bfloat16 [64, 128, 10240], P('blk', None, 'tok')
- grad_right_up: float32 [64, 512, 128], P('blk')
- grad_left_up: float32 [512, 64, 64], P('blk')
- grad_left_down: float32 [512, 64, 64], P('blk')
- grad_right_down: float32 [64, 128, 512], P('blk')
All inputs are finite; a program needn't handle non-finite values.
Results may differ from a plain program's by a relative error of at most 0.0068.
Values may be sent and summed in bfloat16 or wider, within the bound.
A program may use at most 192 MiB of HBM per device.

v0:
```python
import functools

import jax
import jax.numpy as jnp
from jax import lax
from jax.experimental import pallas as pl
from jax.experimental.pallas import tpu as pltpu
from jax.sharding import PartitionSpec as P

MESH = pl.DeviceIdType.MESH
CHUNK = 512
SPAN = 256
ROOT = 0.7978845608028654
CUBIC = 0.044715


def dot(a, b):
    return jnp.dot(a, b, preferred_element_type=jnp.float32)


def dot_nt(a, b):
    return lax.dot_general(a, b, (((1,), (1,)), ((), ())), preferred_element_type=jnp.float32)


def kernel(
    chunks, owners, x_ref, cot_ref, w1_ref, w1t_ref, w2_ref, w2t_ref, w3_ref, w3t_ref, w4_ref, w4t_ref,
    out_ref, gt_ref, sums_ref,
    send_a, send_b, got_first, got_back, got_mixed, got_last, hidden, slope, back_pre,
    acc_ru, acc_rd, acc_ld, acc_lu, grads, near, own, far,
    send_sem, recv_sem, sum_send, sum_recv,
):
    me = lax.axis_index("blk")
    tok = lax.axis_index("tok")
    core_peer = tok + 1 - 2 * lax.rem(tok, 2)
    far_peer = tok + 2 - 4 * (tok // 2)
    rows = send_a.shape[2]
    half = rows // 2
    count = owners - 1

    barrier = pltpu.get_barrier_semaphore()

    def greet(i, carry):
        pl.semaphore_signal(barrier, inc=1, device_id=(tok, lax.rem(me + i, owners)), device_id_type=MESH)
        return carry

    lax.fori_loop(1, owners, greet, 0)
    pl.semaphore_signal(barrier, inc=1, device_id=(core_peer, me), device_id_type=MESH)
    pl.semaphore_signal(barrier, inc=1, device_id=(far_peer, me), device_id_type=MESH)

    for acc in (acc_ru, acc_rd, acc_ld, acc_lu):
        acc[...] = jnp.zeros_like(acc)

    def columns(k):
        return pl.ds(pl.multiple_of(k * CHUNK, CHUNK), CHUNK)

    def post(kind, k, source, target):
        pltpu.make_async_copy(source.at[k, me], target.at[k, me], recv_sem.at[kind, k]).start()

        def one(i, carry):
            to = lax.rem(me + i, owners)
            pltpu.make_async_remote_copy(
                src_ref=source.at[k, to], dst_ref=target.at[k, me],
                send_sem=send_sem.at[kind, k], recv_sem=recv_sem.at[kind, k],
                device_id=(tok, to), device_id_type=MESH,
            ).start()
            return carry

        lax.fori_loop(1, owners, one, 0)

    def sent(kind, k, source):
        part = source.at[k, pl.ds(0, count)]
        pltpu.make_async_copy(part, part, send_sem.at[kind, k]).wait()

    def arrived(kind, k, target):
        pltpu.make_async_copy(target.at[k], target.at[k], recv_sem.at[kind, k]).wait()

    wide = SPAN // rows

    def spread(w_ref, data, buffer, k):
        def part(r, carry):
            w = w_ref[pl.ds(pl.multiple_of(r * SPAN, SPAN), SPAN), :]
            value = dot(w, data).astype(jnp.bfloat16)
            buffer[k, pl.ds(r * wide, wide)] = value.reshape(wide, rows, CHUNK)
            return carry

        lax.fori_loop(0, w_ref.shape[0] // SPAN, part, 0)

    def stage_first(k):
        spread(w1_ref, x_ref[:, columns(k)], send_a, k)

    def stage_back(k):
        spread(w4t_ref, cot_ref[:, columns(k)], send_b, k)

    def rows_of(buffer, k, h):
        return buffer[k, :, h * half:(h + 1) * half, :].reshape(owners * half, CHUNK)

    def keep_block(acc, h, r, value):
        which = lax.rem(lax.broadcasted_iota(jnp.int32, (SPAN, 128), 0), half) // 4
        kept = value[:, 0:128]
        for p in range(1, half // 4):
            kept = jnp.where(which == p, value[:, p * 128:(p + 1) * 128], kept)
        acc[h, r * SPAN:(r + 1) * SPAN, :] += kept

    def stage_middle(k):
        arrived(0, k, got_first)
        sent(0, k, send_a)
        size = owners * half
        for h in range(2):
            given = rows_of(got_first, k, h)
            for r in range(size // SPAN):
                at = pl.ds(r * SPAN, SPAN)
                pre = dot(w2_ref[h, at, :], given)
                square = pre * pre
                t = jnp.tanh(ROOT * (pre + CUBIC * (square * pre)))
                cdf = 0.5 * (1.0 + t)
                hidden[h, at, :] = (pre * cdf).astype(jnp.bfloat16)
                slope[h, at, :] = cdf + (0.5 * ROOT) * pre * (1.0 - t * t) * (1.0 + (3.0 * CUBIC) * square)
        each = SPAN // half
        for h in range(2):
            for r in range(size // SPAN):
                value = dot(w3_ref[h, pl.ds(r * SPAN, SPAN), :], hidden[h]).astype(jnp.bfloat16)
                send_a[k, r * each:(r + 1) * each, h * half:(h + 1) * half, :] = value.reshape(each, half, CHUNK)
        post(2, k, send_a, got_mixed)

        arrived(1, k, got_back)
        sent(1, k, send_b)
        for h in range(2):
            given = rows_of(got_back, k, h)
            for r in range(size // SPAN):
                at = pl.ds(r * SPAN, SPAN)
                back = dot(w3t_ref[h, at, :], given)
                back_pre[h, at, :] = (back * slope[h, at, :]).astype(jnp.bfloat16)
        for h in range(2):
            for r in range(size // SPAN):
                value = dot(w2t_ref[h, pl.ds(r * SPAN, SPAN), :], back_pre[h]).astype(jnp.bfloat16)
                send_b[k, r * each:(r + 1) * each, h * half:(h + 1) * half, :] = value.reshape(each, half, CHUNK)
        post(3, k, send_b, got_last)

        for h in range(2):
            for r in range(size // SPAN):
                part = slice(r * each, (r + 1) * each)
                inner = slice(h * half, (h + 1) * half)
                back = got_back[k, part, inner, :].reshape(SPAN, CHUNK)
                keep_block(acc_ld, h, r, dot_nt(back, hidden[h]))
                first = got_first[k, part, inner, :].reshape(SPAN, CHUNK)
                keep_block(acc_lu, h, r, dot_nt(first, back_pre[h]))

    def gather(k, got, w_ref, data_ref, into_ref, acc):
        data = data_ref[:, columns(k)]
        everything = got[k].reshape(owners * rows, CHUNK)
        into_ref[:, columns(k)] = dot(w_ref[...], everything).astype(jnp.bfloat16)
        odd = lax.rem(lax.broadcasted_iota(jnp.int32, (SPAN, 128), 0), 2) == 1

        def part(r, carry):
            piece = got[k, pl.ds(r * wide, wide)].reshape(SPAN, CHUNK)
            value = dot_nt(piece, data)
            at = pl.ds(pl.multiple_of(r * SPAN, SPAN), SPAN)
            acc[at, :] += jnp.where(odd, value[:, 128:256], value[:, 0:128])
            return carry

        lax.fori_loop(0, owners * rows // SPAN, part, 0)

    def stage_output(k):
        arrived(2, k, got_mixed)
        gather(k, got_mixed, w4_ref, cot_ref, out_ref, acc_rd)

    def stage_grad(k):
        arrived(3, k, got_last)
        gather(k, got_last, w1t_ref, x_ref, gt_ref, acc_ru)

    stage_first(0)
    stage_back(0)
    pl.semaphore_wait(barrier, count + 2)
    post(0, 0, send_a, got_first)
    post(1, 0, send_b, got_back)

    def ahead(k):
        stage_first(k)
        post(0, k, send_a, got_first)
        stage_back(k)
        post(1, k, send_b, got_back)

    ahead(1)

    def step(k, carry):
        stage_middle(k)

        @pl.when(k + 2 < chunks)
        def _():
            ahead(k + 2)

        @pl.when(k >= 1)
        def _():
            stage_output(k - 1)
            stage_grad(k - 1)

        return carry

    lax.fori_loop(0, chunks, step, 0)

    part = grads.shape[1] // 2
    core = lax.rem(tok, 2)
    mine = pl.ds(pl.multiple_of(core * part, part), part)
    theirs = pl.ds(pl.multiple_of(part - core * part, part), part)

    def pair(i):
        return pltpu.make_async_remote_copy(
            src_ref=grads.at[i, theirs], dst_ref=near.at[i], send_sem=sum_send.at[0, i], recv_sem=sum_recv.at[0, i],
            device_id=(core_peer, me), device_id_type=MESH,
        )

    def across(i):
        return pltpu.make_async_remote_copy(
            src_ref=own.at[i], dst_ref=far.at[i], send_sem=sum_send.at[1, i], recv_sem=sum_recv.at[1, i],
            device_id=(far_peer, me), device_id_type=MESH,
        )

    def share(i):
        return pltpu.make_async_remote_copy(
            src_ref=sums_ref.at[i, mine], dst_ref=sums_ref.at[i, mine],
            send_sem=sum_send.at[2, i], recv_sem=sum_recv.at[2, i],
            device_id=(core_peer, me), device_id_type=MESH,
        )

    def begin(i):
        pair(i).start()

    def middle(i):
        pair(i).wait()
        own[i] = grads[i, mine, :] + near[i]
        across(i).start()

    def finish(i):
        across(i).wait()
        sums_ref[i, mine, :] = own[i] + far[i]
        share(i).start()

    lane = lax.broadcasted_iota(jnp.int32, (owners, 128), 1)
    for h in range(2):
        for c in range(half // 2):
            for s in range(2):
                ld = acc_ld[h, pl.ds(2 * c + s, owners, stride=half), :]
                lu = acc_lu[h, pl.ds(2 * c + s, owners, stride=half), :]
                if c % 2 == 0:
                    both = jnp.where(lane < 64, ld, pltpu.roll(lu, 64, 1))
                else:
                    both = jnp.where(lane < 64, pltpu.roll(ld, 64, 1), lu)
                base = (h * (half // 2) + c) * 2 * owners
                grads[0, pl.ds(base + s, owners, stride=2), :] = both
    begin(0)

    size = owners * half
    last = chunks - 1
    stage_output(last)
    for s in range(2):
        grads[1, s * size:(s + 1) * size, :] = acc_rd[pl.ds(s, size, stride=2), :]
    begin(1)
    middle(0)
    middle(1)
    stage_grad(last)
    for s in range(2):
        grads[2, s * size:(s + 1) * size, :] = acc_ru[pl.ds(s, size, stride=2), :]
    begin(2)
    finish(0)
    finish(1)
    middle(2)
    finish(2)

    def drain(k, carry):
        sent(2, k, send_a)
        sent(3, k, send_b)
        return carry

    lax.fori_loop(0, chunks, drain, 0)
    for i in range(3):
        share(i).wait()


def shards(tokens, cotangent, right_up, left_up, left_down, right_down):
    tok_count = lax.axis_size("tok")
    owners = lax.axis_size("blk")
    factor = float(tokens.shape[2] * tok_count) ** (-0.5)
    pair, width, count = tokens.shape
    hidden_blocks = right_up.shape[1]
    own_blocks = left_up.shape[0]
    units = left_up.shape[1]
    eight = own_blocks // 2
    chunks = count // CHUNK
    bf = jnp.bfloat16

    two = jnp.eye(pair, dtype=bf)
    eye = jnp.eye(eight, dtype=bf)
    wide, deep = pair * hidden_blocks, pair * width
    w1 = (right_up.transpose(1, 0, 2)[:, :, None, :] * two[None, :, :, None]).reshape(wide, deep)
    w1t = (right_up.transpose(0, 2, 1)[:, :, :, None] * two[:, None, None, :]).reshape(deep, wide)
    w4 = (right_down[:, :, :, None] * two[:, None, None, :]).reshape(deep, wide)
    w4t = (right_down.transpose(2, 0, 1)[:, :, None, :] * two[None, :, :, None]).reshape(wide, deep)
    size = eight * units
    up = left_up.reshape(2, eight, units, owners, pair)
    w2 = (up[:, :, :, :, None, :] * eye[None, :, None, None, :, None]).reshape(2, size, size)
    w2t = (up.transpose(0, 3, 1, 4, 2)[:, :, :, :, None, :] * eye[None, None, :, None, :, None]).reshape(2, size, size)
    down = left_down.reshape(2, eight, owners, pair, units)
    w3 = (down.transpose(0, 2, 1, 3, 4)[:, :, :, :, None, :] * eye[None, None, :, None, :, None]).reshape(2, size, size)
    w3t = (down.transpose(0, 1, 4, 2, 3)[:, :, :, :, None, :] * eye[None, :, None, None, :, None]).reshape(2, size, size)

    rows = pair * own_blocks
    flow = pltpu.VMEM((chunks, owners, rows, CHUNK), bf)
    vmem = pl.BlockSpec(memory_space=pltpu.VMEM)
    output, grad_tokens, sums = pl.pallas_call(
        functools.partial(kernel, chunks, owners),
        out_shape=(
            jax.ShapeDtypeStruct((deep, count), bf),
            jax.ShapeDtypeStruct((deep, count), bf),
            jax.ShapeDtypeStruct((3, wide, 128), jnp.float32),
        ),
        in_specs=[vmem] * 10,
        out_specs=(vmem, vmem, vmem),
        scratch_shapes=[
            flow, flow, flow, flow, flow, flow,
            pltpu.VMEM((2, size, CHUNK), bf),
            pltpu.VMEM((2, size, CHUNK), jnp.float32),
            pltpu.VMEM((2, size, CHUNK), bf),
            pltpu.VMEM((wide, 128), jnp.float32),
            pltpu.VMEM((wide, 128), jnp.float32),
            pltpu.VMEM((2, size, 128), jnp.float32),
            pltpu.VMEM((2, size, 128), jnp.float32),
            pltpu.VMEM((3, wide, 128), jnp.float32),
            pltpu.VMEM((3, wide // 2, 128), jnp.float32),
            pltpu.VMEM((3, wide // 2, 128), jnp.float32),
            pltpu.VMEM((3, wide // 2, 128), jnp.float32),
            pltpu.SemaphoreType.DMA((4, chunks)),
            pltpu.SemaphoreType.DMA((4, chunks)),
            pltpu.SemaphoreType.DMA((3, 3)),
            pltpu.SemaphoreType.DMA((3, 3)),
        ],
        compiler_params=pltpu.CompilerParams(
            collective_id=0, has_side_effects=True, vmem_limit_bytes=60 << 20
        ),
        name="monarch",
    )(
        tokens.reshape(deep, count), cotangent.reshape(deep, count),
        w1, w1t, w2, w2t, w3, w3t, w4, w4t,
    )
    sums = sums * factor
    both = sums[0].reshape(own_blocks, units, 128)
    grad_ld = both[:, :, :units]
    grad_lu = both[:, :, units:].transpose(0, 2, 1)
    grad_rd = sums[1].reshape(pair, hidden_blocks, width).transpose(0, 2, 1)
    grad_ru = sums[2].reshape(pair, hidden_blocks, width)
    shape = tokens.shape
    return (output.reshape(shape), grad_tokens.reshape(shape), grad_ru, grad_lu, grad_ld, grad_rd)


def solution(mesh):
    split = P("blk", None, "tok")
    whole = P("blk", None, None)
    return jax.shard_map(
        shards,
        mesh=mesh,
        in_specs=(split, split, whole, whole, whole, whole),
        out_specs=(split, split, whole, whole, whole, whole),
        check_vma=False,
    )
```

profile of v0, /device:TPU:1, one launch (start us, length us, event | category | flops | bytes accessed | tf_op | source)
XLA Modules:
  0.0 373.5 jit_solution(12875798086693361944)
XLA Ops:
  0.6 0.0 copy-start.6
  0.6 0.0 copy-start.4
  0.7 0.1 copy.21
  0.8 0.1 copy.28
  0.9 1.2 copy.23
  2.2 0.9 copy.27
  3.1 0.0 copy-done.6
  3.1 0.2 copy.33
  3.2 0.0 copy-done.4
  3.3 1.0 copy.30
  4.3 0.9 copy.29
  5.1 0.0 copy-done.5
  5.1 0.3 copy.20
  5.4 0.3 copy.22
  5.7 0.2 copy.32
  5.9 0.9 broadcast_multiply_fusion.6
  6.8 0.1 copy.46
  6.8 1.0 copy.35.w4_ref
  7.9 0.1 copy.47
  7.9 1.0 copy.34.w1t_ref
  8.9 1.1 broadcast_multiply_fusion.5
  10.1 1.1 copy_bitcast_fusion
  11.2 0.3 mul.167
  11.5 0.6 mul.168
  12.1 1.0 copy.25
  13.2 0.3 mul.173
  13.5 1.4 mul.174
  14.9 1.5 mul.177
  16.4 1.4 mul.178
  17.9 1.2 mul.180
  19.1 2.0 mul.181
  21.1 2.3 copy.31
  23.4 1.5 mul.171
  24.9 2.0 mul.172
  27.0 0.3 mul.165
  27.3 2.0 mul.166
  29.3 2.4 copy.26
  31.7 0.0 copy-done
  31.7 3.6 broadcast_multiply_fusion.1
  35.4 329.9 %monarch.1 = (bf16[256,2560]{1,0:T(8,128)(2,1)}, bf16[256,2560]{1,0:T(8,128)(2,1)}, f32[3,1024,128]{2,1,0:T(8,128)}) custom-call(bf16[256,2560]{1,0:T(8,128)(2,1)} %bitcast.71, bf16[256,2560]{1,0:T(8,128)(2,1)} %bitcast.72, bf16[1024,256]{1,0:T(8,128)(2,1)} %get-tuple-element.38.w1_ref, bf16[256,1024]{1,0:T(8,128)(2,1)} %copy.34.w1t_ref, ...), custom_call_target="tpu_custom_call" | custom-call | tf_op jit(solution)/shard_map/monarch/pallas_call | solution.py:309
  365.3 1.5 broadcast_multiply_fusion
  366.9 0.9 fusion.1
  367.8 1.0 copy.36
  368.8 0.9 fusion.2
  369.7 1.0 copy.37
  370.7 1.1 copy.50
  371.7 0.7 copy-done.2
  372.5 1.1 copy.51
  (10 shorter events, 0.1 us)
Async XLA Ops:
  0.6 2.4 copy-start.6
  0.6 2.6 copy-start.4
  0.9 4.3 %copy-start.5 = (bf16[2,512,128]{2,1,0:T(8,128)(2,1)S(1)}, bf16[2,512,128]{2,1,0:T(8,128)(2,1)}, u32[]{:S(2)}) copy-start(bf16[2,512,128]{2,1,0:T(8,128)(2,1)} %param.8) | copy-start | bytes 786436
  29.3 2.4 copy-start
  29.3 2.4 copy-start.1
  368.8 1.9 copy-start.3
  370.7 1.8 copy-start.2
where the time goes:
time: 374 us
  Pallas kernels  330 us (88%)
  local copies, waits for them, and re-layouts  35.6 us (10%)
  other arithmetic  7.17 us (2%)
    pallas_call x1, Pallas kernels, shards(): pl.pallas_call(functools.partial(kernel, chunks, owners), out_shape=(jax....  330 us

commit v1 on v0

--- a/solution.py
+++ b/solution.py
@@ -22,9 +22,36 @@
     return lax.dot_general(a, b, (((1,), (1,)), ((), ())), preferred_element_type=jnp.float32)
 
 
+def hops():
+    near = lambda v: min(v, 4 - v)
+    steps = [(x, z, y) for x in range(4) for z in range(4) for y in range(2)][1:]
+    order = []
+    for step in sorted(steps, key=lambda s: -(near(s[0]) + near(s[1]) + s[2])):
+        for x, z in ((step[0], step[1]), (step[1], step[0])):
+            for twin in ((x, z, step[2]), (-x % 4, -z % 4, step[2])):
+                if twin not in order:
+                    order.append(twin)
+    return order
+
+
+def neighbour(me, step):
+    x, z, y = me // 8, lax.rem(me // 2, 4), lax.rem(me, 2)
+    return (lax.rem(x + step[0], 4) * 4 + lax.rem(z + step[1], 4)) * 2 + lax.rem(y + step[2], 2)
+
+
+def one_hot(test):
+    return jnp.where(test, 1.0, 0.0).astype(jnp.bfloat16)
+
+
+def square(size):
+    row = lax.broadcasted_iota(jnp.int32, (size, size), 0)
+    return one_hot(row == lax.broadcasted_iota(jnp.int32, (size, size), 1))
+
+
 def kernel(
-    chunks, owners, x_ref, cot_ref, w1_ref, w1t_ref, w2_ref, w2t_ref, w3_ref, w3t_ref, w4_ref, w4t_ref,
+    chunks, owners, x_ref, cot_ref, ru_ref, lu_ref, ld_ref, rd_ref,
     out_ref, gt_ref, sums_ref,
+    w1_ref, w1t_ref, w2_ref, w2t_ref, w3_ref, w3t_ref, w4_ref, w4t_ref,
     send_a, send_b, got_first, got_back, got_mixed, got_last, hidden, slope, back_pre,
     acc_ru, acc_rd, acc_ld, acc_lu, grads, near, own, far,
     send_sem, recv_sem, sum_send, sum_recv,
@@ -36,36 +63,72 @@
     rows = send_a.shape[2]
     half = rows // 2
     count = owners - 1
+    others = [neighbour(me, step) for step in hops()]
 
     barrier = pltpu.get_barrier_semaphore()
 
-    def greet(i, carry):
-        pl.semaphore_signal(barrier, inc=1, device_id=(tok, lax.rem(me + i, owners)), device_id_type=MESH)
-        return carry
-
-    lax.fori_loop(1, owners, greet, 0)
+    for to in others:
+        pl.semaphore_signal(barrier, inc=1, device_id=(tok, to), device_id_type=MESH)
     pl.semaphore_signal(barrier, inc=1, device_id=(core_peer, me), device_id_type=MESH)
     pl.semaphore_signal(barrier, inc=1, device_id=(far_peer, me), device_id_type=MESH)
 
     for acc in (acc_ru, acc_rd, acc_ld, acc_lu):
         acc[...] = jnp.zeros_like(acc)
 
+    def interleave():
+        row = lax.broadcasted_iota(jnp.int32, (SPAN, SPAN // 2), 0)
+        spot = 2 * lax.broadcasted_iota(jnp.int32, (SPAN, SPAN // 2), 1)
+        for s in range(2):
+            pick = one_hot(row == spot + s)
+            for r in range(w1_ref.shape[0] // SPAN):
+                at, part = slice(r * SPAN, (r + 1) * SPAN), slice(r * SPAN // 2, (r + 1) * SPAN // 2)
+                lanes = slice(s * 128, (s + 1) * 128)
+                w1_ref[at, lanes] = dot(pick, ru_ref[s, part, :]).astype(jnp.bfloat16)
+                w4t_ref[at, lanes] = dot_nt(pick, rd_ref[s, :, part]).astype(jnp.bfloat16)
+
+    def turned():
+        flip = square(SPAN)
+        for r in range(w1_ref.shape[0] // SPAN):
+            at = slice(r * SPAN, (r + 1) * SPAN)
+            w1t_ref[:, at] = dot_nt(flip, w1_ref[at, :]).astype(jnp.bfloat16)
+            w4_ref[:, at] = dot_nt(flip, w4t_ref[at, :]).astype(jnp.bfloat16)
+
+    def expand():
+        units = lu_ref.shape[1]
+        size = owners * half
+        row = lax.broadcasted_iota(jnp.int32, (units, size), 0)
+        col = lax.broadcasted_iota(jnp.int32, (units, size), 1)
+        same = row == 2 * (col // half) + lax.rem(col, 2)
+        block = lax.rem(col, half) // 2
+        small = square(units)
+        flip = square(SPAN)
+        for c in range(half // 2):
+            place = one_hot(same & (block == c))
+            at = slice(c * units, (c + 1) * units)
+            for h in range(2):
+                index = h * (half // 2) + c
+                w2_ref[h, at, :] = dot(lu_ref[index], place).astype(jnp.bfloat16)
+                down = dot_nt(small, ld_ref[index]).astype(jnp.bfloat16)
+                w3t_ref[h, at, :] = dot(down, place).astype(jnp.bfloat16)
+        for h in range(2):
+            for r in range(size // SPAN):
+                for q in range(size // SPAN):
+                    at, to = slice(r * SPAN, (r + 1) * SPAN), slice(q * SPAN, (q + 1) * SPAN)
+                    w2t_ref[h, to, at] = dot_nt(flip, w2_ref[h, at, to]).astype(jnp.bfloat16)
+                    w3_ref[h, to, at] = dot_nt(flip, w3t_ref[h, at, to]).astype(jnp.bfloat16)
+
     def columns(k):
         return pl.ds(pl.multiple_of(k * CHUNK, CHUNK), CHUNK)
 
     def post(kind, k, source, target):
         pltpu.make_async_copy(source.at[k, me], target.at[k, me], recv_sem.at[kind, k]).start()
 
-        def one(i, carry):
-            to = lax.rem(me + i, owners)
+        for to in others:
             pltpu.make_async_remote_copy(
                 src_ref=source.at[k, to], dst_ref=target.at[k, me],
                 send_sem=send_sem.at[kind, k], recv_sem=recv_sem.at[kind, k],
                 device_id=(tok, to), device_id_type=MESH,
             ).start()
-            return carry
-
-        lax.fori_loop(1, owners, one, 0)
 
     def sent(kind, k, source):
         part = source.at[k, pl.ds(0, count)]
@@ -168,6 +231,7 @@
         arrived(3, k, got_last)
         gather(k, got_last, w1t_ref, x_ref, gt_ref, acc_ru)
 
+    interleave()
     stage_first(0)
     stage_back(0)
     pl.semaphore_wait(barrier, count + 2)
@@ -181,6 +245,8 @@
         post(1, k, send_b, got_back)
 
     ahead(1)
+    expand()
+    turned()
 
     def step(k, carry):
         stage_middle(k)
@@ -288,21 +354,8 @@
     chunks = count // CHUNK
     bf = jnp.bfloat16
 
-    two = jnp.eye(pair, dtype=bf)
-    eye = jnp.eye(eight, dtype=bf)
     wide, deep = pair * hidden_blocks, pair * width
-    w1 = (right_up.transpose(1, 0, 2)[:, :, None, :] * two[None, :, :, None]).reshape(wide, deep)
-    w1t = (right_up.transpose(0, 2, 1)[:, :, :, None] * two[:, None, None, :]).reshape(deep, wide)
-    w4 = (right_down[:, :, :, None] * two[:, None, None, :]).reshape(deep, wide)
-    w4t = (right_down.transpose(2, 0, 1)[:, :, None, :] * two[None, :, :, None]).reshape(wide, deep)
     size = eight * units
-    up = left_up.reshape(2, eight, units, owners, pair)
-    w2 = (up[:, :, :, :, None, :] * eye[None, :, None, None, :, None]).reshape(2, size, size)
-    w2t = (up.transpose(0, 3, 1, 4, 2)[:, :, :, :, None, :] * eye[None, None, :, None, :, None]).reshape(2, size, size)
-    down = left_down.reshape(2, eight, owners, pair, units)
-    w3 = (down.transpose(0, 2, 1, 3, 4)[:, :, :, :, None, :] * eye[None, None, :, None, :, None]).reshape(2, size, size)
-    w3t = (down.transpose(0, 1, 4, 2, 3)[:, :, :, :, None, :] * eye[None, :, None, None, :, None]).reshape(2, size, size)
-
     rows = pair * own_blocks
     flow = pltpu.VMEM((chunks, owners, rows, CHUNK), bf)
     vmem = pl.BlockSpec(memory_space=pltpu.VMEM)
@@ -313,9 +366,13 @@
             jax.ShapeDtypeStruct((deep, count), bf),
             jax.ShapeDtypeStruct((3, wide, 128), jnp.float32),
         ),
-        in_specs=[vmem] * 10,
+        in_specs=[vmem] * 6,
         out_specs=(vmem, vmem, vmem),
         scratch_shapes=[
+            pltpu.VMEM((wide, deep), bf), pltpu.VMEM((deep, wide), bf),
+            pltpu.VMEM((2, size, size), bf), pltpu.VMEM((2, size, size), bf),
+            pltpu.VMEM((2, size, size), bf), pltpu.VMEM((2, size, size), bf),
+            pltpu.VMEM((deep, wide), bf), pltpu.VMEM((wide, deep), bf),
             flow, flow, flow, flow, flow, flow,
             pltpu.VMEM((2, size, CHUNK), bf),
             pltpu.VMEM((2, size, CHUNK), jnp.float32),
@@ -339,7 +396,7 @@
         name="monarch",
     )(
         tokens.reshape(deep, count), cotangent.reshape(deep, count),
-        w1, w1t, w2, w2t, w3, w3t, w4, w4t,
+        right_up, left_up, left_down, right_down,
     )
     sums = sums * factor
     both = sums[0].reshape(own_blocks, units, 128)

time: 374 us -> 270 us (0.72)
  Pallas kernels: 330 us -> 261 us
  local copies, waits for them, and re-layouts: 35.6 us -> 6.67 us
  other arithmetic: 7.17 us -> 1.54 us
    pallas_call x1, Pallas kernels: 330 us -> 261 us  [shards(): pl.pallas_call(functools.partial(kernel, chunks, owners), out_shape=(jax....]
    mul x19 -> x0, local copies, waits for them, and re-layouts: 23.7 us -> none  [the longest x7 6.74 us: shards(): up[:, :, :, :, None, :] * eye[None, :, None, None, :, None]]
    mul x3 -> x0, other arithmetic: 5.61 us -> none  [the longest x1 3.62 us: shards(): down.transpose(0, 2, 1, 3, 4)[:, :, :, :, None, :]]
where the time goes in v1:
time: 270 us
  Pallas kernels  261 us (97%)
  local copies, waits for them, and re-layouts  6.67 us (2%)
    pallas_call x1, Pallas kernels, shards(): pl.pallas_call(functools.partial(kernel, chunks, owners), out_shape=(jax....  261 us

profile of v1, /device:TPU:1, one launch (start us, length us, event | category | flops | bytes accessed | tf_op | source)
XLA Modules:
  0.0 269.6 jit_solution(13404101509375128305)
XLA Ops:
  0.6 260.7 %monarch.1 = (bf16[256,2560]{1,0:T(8,128)(2,1)}, bf16[256,2560]{1,0:T(8,128)(2,1)}, f32[3,1024,128]{2,1,0:T(8,128)}) custom-call(bf16[256,2560]{1,0:T(8,128)(2,1)} %bitcast.12, bf16[256,2560]{1,0:T(8,128)(2,1)} %bitcast.13, bf16[2,512,128]{2,1,0:T(8,128)(2,1)} %ru_ref.1, bf16[16,64,64]{2,1,0:T(8,128)(2,1)} %lu_ref.1, bf16[16,64,64]{2,1,0:T(8,128)(2,1)} %ld_ref.1, ...), custom_call_target="tpu_custom_call" | custom-call | tf_op jit(solution)/shard_map/monarch/pallas_call | solution.py:362
  261.4 1.5 broadcast_multiply_fusion
  262.9 0.9 fusion
  263.8 1.0 copy.12
  264.8 0.0 copy-start.1
  264.8 0.9 fusion.1
  265.8 1.0 copy.13
  266.8 0.0 copy-done.1
  266.8 0.0 copy-start
  266.8 1.1 copy.16
  267.8 0.7 copy-done
  268.6 1.1 copy.17
Async XLA Ops:
  264.8 1.9 copy-start.1
  266.8 1.8 copy-start

commit v2 on v1

--- a/solution.py
+++ b/solution.py
@@ -8,7 +8,9 @@
 from jax.sharding import PartitionSpec as P
 
 MESH = pl.DeviceIdType.MESH
-CHUNK = 512
+CHUNK = 256
+AHEAD = 4
+LAG = 2
 SPAN = 256
 ROOT = 0.7978845608028654
 CUBIC = 0.044715
@@ -49,12 +51,13 @@
 
 
 def kernel(
-    chunks, owners, x_ref, cot_ref, ru_ref, lu_ref, ld_ref, rd_ref,
-    out_ref, gt_ref, sums_ref,
+    chunks, owners, x_hbm, cot_hbm, ru_ref, rd_ref, lu_hbm, ld_hbm,
+    out_hbm, gt_hbm, sums_ref,
+    x_ref, cot_ref, lu_ref, ld_ref, out_ref, gt_ref,
     w1_ref, w1t_ref, w2_ref, w2t_ref, w3_ref, w3t_ref, w4_ref, w4t_ref,
     send_a, send_b, got_first, got_back, got_mixed, got_last, hidden, slope, back_pre,
     acc_ru, acc_rd, acc_ld, acc_lu, grads, near, own, far,
-    send_sem, recv_sem, sum_send, sum_recv,
+    send_sem, recv_sem, sum_send, sum_recv, in_sem, out_sem,
 ):
     me = lax.axis_index("blk")
     tok = lax.axis_index("tok")
@@ -65,15 +68,27 @@
     count = owners - 1
     others = [neighbour(me, step) for step in hops()]
 
+    def columns(k):
+        return pl.ds(pl.multiple_of(k * CHUNK, CHUNK), CHUNK)
+
+    head, tail = pl.ds(0, CHUNK), pl.ds(CHUNK, x_ref.shape[1] - CHUNK)
+    loads = [
+        pltpu.make_async_copy(x_hbm.at[:, head], x_ref.at[:, head], in_sem.at[0]),
+        pltpu.make_async_copy(cot_hbm.at[:, head], cot_ref.at[:, head], in_sem.at[1]),
+        pltpu.make_async_copy(x_hbm.at[:, tail], x_ref.at[:, tail], in_sem.at[2]),
+        pltpu.make_async_copy(cot_hbm.at[:, tail], cot_ref.at[:, tail], in_sem.at[3]),
+        pltpu.make_async_copy(lu_hbm, lu_ref, in_sem.at[4]),
+        pltpu.make_async_copy(ld_hbm, ld_ref, in_sem.at[5]),
+    ]
+    for load in loads:
+        load.start()
+
     barrier = pltpu.get_barrier_semaphore()
 
     for to in others:
         pl.semaphore_signal(barrier, inc=1, device_id=(tok, to), device_id_type=MESH)
     pl.semaphore_signal(barrier, inc=1, device_id=(core_peer, me), device_id_type=MESH)
     pl.semaphore_signal(barrier, inc=1, device_id=(far_peer, me), device_id_type=MESH)
-
-    for acc in (acc_ru, acc_rd, acc_ld, acc_lu):
-        acc[...] = jnp.zeros_like(acc)
 
     def interleave():
         row = lax.broadcasted_iota(jnp.int32, (SPAN, SPAN // 2), 0)
@@ -117,9 +132,6 @@
                     w2t_ref[h, to, at] = dot_nt(flip, w2_ref[h, at, to]).astype(jnp.bfloat16)
                     w3_ref[h, to, at] = dot_nt(flip, w3t_ref[h, at, to]).astype(jnp.bfloat16)
 
-    def columns(k):
-        return pl.ds(pl.multiple_of(k * CHUNK, CHUNK), CHUNK)
-
     def post(kind, k, source, target):
         pltpu.make_async_copy(source.at[k, me], target.at[k, me], recv_sem.at[kind, k]).start()
 
@@ -208,10 +220,12 @@
                 first = got_first[k, part, inner, :].reshape(SPAN, CHUNK)
                 keep_block(acc_lu, h, r, dot_nt(first, back_pre[h]))
 
-    def gather(k, got, w_ref, data_ref, into_ref, acc):
-        data = data_ref[:, columns(k)]
+    def apply(k, got, w_ref, into_ref):
         everything = got[k].reshape(owners * rows, CHUNK)
         into_ref[:, columns(k)] = dot(w_ref[...], everything).astype(jnp.bfloat16)
+
+    def collect(k, got, data_ref, acc):
+        data = data_ref[:, columns(k)]
         odd = lax.rem(lax.broadcasted_iota(jnp.int32, (SPAN, 128), 0), 2) == 1
 
         def part(r, carry):
@@ -223,20 +237,38 @@
 
         lax.fori_loop(0, owners * rows // SPAN, part, 0)
 
+    def save_out(k):
+        return pltpu.make_async_copy(out_ref.at[:, columns(k)], out_hbm.at[:, columns(k)], out_sem.at[0, k])
+
+    def save_gt(k):
+        return pltpu.make_async_copy(gt_ref.at[:, columns(k)], gt_hbm.at[:, columns(k)], out_sem.at[1, k])
+
     def stage_output(k):
+        apply(k, got_mixed, w4_ref, out_ref)
+        save_out(k).start()
+
+    def stage_grad(k):
+        apply(k, got_last, w1t_ref, gt_ref)
+        save_gt(k).start()
+
+    def sum_output(k):
         arrived(2, k, got_mixed)
-        gather(k, got_mixed, w4_ref, cot_ref, out_ref, acc_rd)
-
-    def stage_grad(k):
+        collect(k, got_mixed, cot_ref, acc_rd)
+
+    def sum_grad(k):
         arrived(3, k, got_last)
-        gather(k, got_last, w1t_ref, x_ref, gt_ref, acc_ru)
+        collect(k, got_last, x_ref, acc_ru)
 
     interleave()
+    loads[0].wait()
     stage_first(0)
+    loads[1].wait()
     stage_back(0)
     pl.semaphore_wait(barrier, count + 2)
     post(0, 0, send_a, got_first)
     post(1, 0, send_b, got_back)
+    loads[2].wait()
+    loads[3].wait()
 
     def ahead(k):
         stage_first(k)
@@ -244,21 +276,28 @@
         stage_back(k)
         post(1, k, send_b, got_back)
 
-    ahead(1)
+    for k in range(1, AHEAD):
+        ahead(k)
+    for acc in (acc_ru, acc_rd, acc_ld, acc_lu):
+        acc[...] = jnp.zeros_like(acc)
+    loads[4].wait()
+    loads[5].wait()
     expand()
     turned()
 
     def step(k, carry):
         stage_middle(k)
 
-        @pl.when(k + 2 < chunks)
+        @pl.when(k + AHEAD < chunks)
         def _():
-            ahead(k + 2)
-
-        @pl.when(k >= 1)
+            ahead(k + AHEAD)
+
+        @pl.when(k >= LAG)
         def _():
-            stage_output(k - 1)
-            stage_grad(k - 1)
+            sum_output(k - LAG)
+            stage_output(k - LAG)
+            sum_grad(k - LAG)
+            stage_grad(k - LAG)
 
         return carry
 
@@ -293,12 +332,12 @@
 
     def middle(i):
         pair(i).wait()
-        own[i] = grads[i, mine, :] + near[i]
+        own[i] = (grads[i, mine, :] + near[i]).astype(jnp.bfloat16)
         across(i).start()
 
     def finish(i):
         across(i).wait()
-        sums_ref[i, mine, :] = own[i] + far[i]
+        sums_ref[i, mine, :] = own[i].astype(jnp.float32) + far[i].astype(jnp.float32)
         share(i).start()
 
     lane = lax.broadcasted_iota(jnp.int32, (owners, 128), 1)
@@ -317,29 +356,56 @@
 
     size = owners * half
     last = chunks - 1
-    stage_output(last)
+    for k in range(chunks - LAG, last):
+        sum_output(k)
+        stage_output(k)
+        sum_grad(k)
+        stage_grad(k)
+    sum_output(last)
     for s in range(2):
         grads[1, s * size:(s + 1) * size, :] = acc_rd[pl.ds(s, size, stride=2), :]
     begin(1)
     middle(0)
+    stage_output(last)
     middle(1)
-    stage_grad(last)
+    sum_grad(last)
     for s in range(2):
         grads[2, s * size:(s + 1) * size, :] = acc_ru[pl.ds(s, size, stride=2), :]
     begin(2)
+    stage_grad(last)
+    middle(2)
     finish(0)
     finish(1)
-    middle(2)
     finish(2)
 
     def drain(k, carry):
         sent(2, k, send_a)
         sent(3, k, send_b)
+        save_out(k).wait()
+        save_gt(k).wait()
         return carry
 
     lax.fori_loop(0, chunks, drain, 0)
     for i in range(3):
         share(i).wait()
+
+
+def finish(factor, out_hbm, gt_hbm, sums_ref, out_to, gt_to, ru_ref, lu_ref, ld_ref, rd_ref, sem):
+    copies = [pltpu.make_async_copy(out_hbm, out_to, sem.at[0]), pltpu.make_async_copy(gt_hbm, gt_to, sem.at[1])]
+    for copy in copies:
+        copy.start()
+    units = ld_ref.shape[1]
+    size = sums_ref.shape[1] // 2
+    for c in range(ld_ref.shape[0]):
+        both = sums_ref[0, c * units:(c + 1) * units, :] * factor
+        ld_ref[c] = both[:, :units]
+        lu_ref[c] = both.T[units:, :]
+    for s in range(2):
+        part = slice(s * size, (s + 1) * size)
+        rd_ref[s] = (sums_ref[1, part, :] * factor).T
+        ru_ref[s] = sums_ref[2, part, :] * factor
+    for copy in copies:
+        copy.wait()
 
 
 def shards(tokens, cotangent, right_up, left_up, left_down, right_down):
@@ -359,6 +425,7 @@
     rows = pair * own_blocks
     flow = pltpu.VMEM((chunks, owners, rows, CHUNK), bf)
     vmem = pl.BlockSpec(memory_space=pltpu.VMEM)
+    hbm = pl.BlockSpec(memory_space=pltpu.HBM)
     output, grad_tokens, sums = pl.pallas_call(
         functools.partial(kernel, chunks, owners),
         out_shape=(
@@ -366,9 +433,12 @@
             jax.ShapeDtypeStruct((deep, count), bf),
             jax.ShapeDtypeStruct((3, wide, 128), jnp.float32),
         ),
-        in_specs=[vmem] * 6,
-        out_specs=(vmem, vmem, vmem),
+        in_specs=[hbm, hbm, vmem, vmem, hbm, hbm],
+        out_specs=(hbm, hbm, vmem),
         scratch_shapes=[
+            pltpu.VMEM((deep, count), bf), pltpu.VMEM((deep, count), bf),
+            pltpu.VMEM(left_up.shape, bf), pltpu.VMEM(left_down.shape, bf),
+            pltpu.VMEM((deep, count), bf), pltpu.VMEM((deep, count), bf),
             pltpu.VMEM((wide, deep), bf), pltpu.VMEM((deep, wide), bf),
             pltpu.VMEM((2, size, size), bf), pltpu.VMEM((2, size, size), bf),
             pltpu.VMEM((2, size, size), bf), pltpu.VMEM((2, size, size), bf),
@@ -383,12 +453,14 @@
             pltpu.VMEM((2, size, 128), jnp.float32),
             pltpu.VMEM((3, wide, 128), jnp.float32),
             pltpu.VMEM((3, wide // 2, 128), jnp.float32),
-            pltpu.VMEM((3, wide // 2, 128), jnp.float32),
-            pltpu.VMEM((3, wide // 2, 128), jnp.float32),
+            pltpu.VMEM((3, wide // 2, 128), bf),
+            pltpu.VMEM((3, wide // 2, 128), bf),
             pltpu.SemaphoreType.DMA((4, chunks)),
             pltpu.SemaphoreType.DMA((4, chunks)),
             pltpu.SemaphoreType.DMA((3, 3)),
             pltpu.SemaphoreType.DMA((3, 3)),
+            pltpu.SemaphoreType.DMA((6,)),
+            pltpu.SemaphoreType.DMA((2, chunks)),
         ],
         compiler_params=pltpu.CompilerParams(
             collective_id=0, has_side_effects=True, vmem_limit_bytes=60 << 20
@@ -396,15 +468,25 @@
         name="monarch",
     )(
         tokens.reshape(deep, count), cotangent.reshape(deep, count),
-        right_up, left_up, left_down, right_down,
+        right_up, right_down, left_up, left_down,
     )
-    sums = sums * factor
-    both = sums[0].reshape(own_blocks, units, 128)
-    grad_ld = both[:, :, :units]
-    grad_lu = both[:, :, units:].transpose(0, 2, 1)
-    grad_rd = sums[1].reshape(pair, hidden_blocks, width).transpose(0, 2, 1)
-    grad_ru = sums[2].reshape(pair, hidden_blocks, width)
     shape = tokens.shape
+    output, grad_tokens, grad_ru, grad_lu, grad_ld, grad_rd = pl.pallas_call(
+        functools.partial(finish, factor),
+        out_shape=(
+            jax.ShapeDtypeStruct((deep, count), bf),
+            jax.ShapeDtypeStruct((deep, count), bf),
+            jax.ShapeDtypeStruct(right_up.shape, jnp.float32),
+            jax.ShapeDtypeStruct(left_up.shape, jnp.float32),
+            jax.ShapeDtypeStruct(left_down.shape, jnp.float32),
+            jax.ShapeDtypeStruct(right_down.shape, jnp.float32),
+        ),
+        in_specs=[hbm, hbm, vmem],
+        out_specs=(hbm, hbm, vmem, vmem, vmem, vmem),
+        scratch_shapes=[pltpu.SemaphoreType.DMA((2,))],
+        compiler_params=pltpu.CompilerParams(vmem_limit_bytes=16 << 20),
+        name="finish",
+    )(output, grad_tokens, sums)
     return (output.reshape(shape), grad_tokens.reshape(shape), grad_ru, grad_lu, grad_ld, grad_rd)
 
 

time: 270 us -> 258 us (0.956)
  Pallas kernels: 261 us -> 253 us
    pallas_call x1, Pallas kernels: 261 us -> 250 us  [shards(): pl.pallas_call(functools.partial(kernel, chunks, owners), out_shape=(jax....]
    pallas_call x0 -> x1, Pallas kernels: none -> 2.84 us  [shards(): pl.pallas_call(functools.partial(finish, factor), out_shape=(jax.ShapeDty...]
where the time goes in v2:
time: 258 us; the launch traced here: 257 us
  Pallas kernels  253 us (98%)
  local copies, waits for them, and re-layouts  4.03 us (2%)
    pallas_call x1, Pallas kernels, shards(): pl.pallas_call(functools.partial(kernel, chunks, owners), out_shape=(jax....  250 us

profile of v2, /device:TPU:1, one launch (start us, length us, event | category | flops | bytes accessed | tf_op | source)
XLA Modules:
  0.0 257.4 jit_solution(13089840412606761231)
XLA Ops:
  0.6 249.9 %monarch.1 = (bf16[256,2560]{1,0:T(8,128)(2,1)}, bf16[256,2560]{1,0:T(8,128)(2,1)}, f32[3,1024,128]{2,1,0:T(8,128)}) custom-call(bf16[256,2560]{1,0:T(8,128)(2,1)} %bitcast.4, bf16[256,2560]{1,0:T(8,128)(2,1)} %bitcast.5, bf16[2,512,128]{2,1,0:T(8,128)(2,1)} %ru_ref.1, bf16[2,128,512]{2,1,0:T(8,128)(2,1)} %rd_ref.1, bf16[16,64,64]{2,1,0:T(8,128)(2,1)} %lu_hbm.1, ...), custom_call_target="tpu_custom_call" | custom-call | tf_op jit(solution)/shard_map/monarch/pallas_call | solution.py:429
  250.5 0.0 copy-start
  250.5 1.4 copy-done
  251.9 0.0 copy-start.1
  251.9 1.3 copy-done.1
  253.3 0.0 copy-start.2
  253.3 1.3 copy-done.2
  254.6 2.8 %finish.1 = (bf16[256,2560]{1,0:T(8,128)(2,1)}, bf16[256,2560]{1,0:T(8,128)(2,1)}, f32[2,512,128]{2,1,0:T(8,128)}, f32[16,64,64]{2,1,0:T(8,128)}, f32[16,64,64]{2,1,0:T(8,128)}, /*index=5*/f32[2,128,512]{2,1,0:T(8,128)}) custom-call(bf16[256,2560]{1,0:T(8,128)(2,1)S(1)} %copy-done.1, bf16[256,2560]{1,0:T(8,128)(2,1)S(1)} %copy-done.2, ...), custom_call_target="tpu_custom_call" | custom-call | tf_op jit(solution)/shard_map/finish/pallas_call | solution.py:474
Async XLA Ops:
  250.5 1.4 copy-start
  251.9 1.3 copy-start.1
  253.3 1.3 copy-start.2

commit v3 on v2

--- a/solution.py
+++ b/solution.py
@@ -52,12 +52,12 @@
 
 def kernel(
     chunks, owners, x_hbm, cot_hbm, ru_ref, rd_ref, lu_hbm, ld_hbm,
-    out_hbm, gt_hbm, sums_ref,
+    out_hbm, gt_hbm, sums_hbm,
     x_ref, cot_ref, lu_ref, ld_ref, out_ref, gt_ref,
     w1_ref, w1t_ref, w2_ref, w2t_ref, w3_ref, w3t_ref, w4_ref, w4t_ref,
     send_a, send_b, got_first, got_back, got_mixed, got_last, hidden, slope, back_pre,
-    acc_ru, acc_rd, acc_ld, acc_lu, grads, near, own, far,
-    send_sem, recv_sem, sum_send, sum_recv, in_sem, out_sem,
+    acc_ru, acc_rd, acc_ld, acc_lu, grads, near, own, far, sums_ref,
+    send_sem, recv_sem, sum_send, sum_recv, in_sem, out_sem, save_sem,
 ):
     me = lax.axis_index("blk")
     tok = lax.axis_index("tok")
@@ -327,6 +327,13 @@
             device_id=(core_peer, me), device_id_type=MESH,
         )
 
+    def save(i):
+        return pltpu.make_async_copy(sums_ref.at[i], sums_hbm.at[i], save_sem.at[i])
+
+    def settle(i):
+        share(i).wait()
+        save(i).start()
+
     def begin(i):
         pair(i).start()
 
@@ -376,8 +383,11 @@
     middle(2)
     finish(0)
     finish(1)
+    settle(0)
+    settle(1)
     finish(2)
 
+    settle(2)
     def drain(k, carry):
         sent(2, k, send_a)
         sent(3, k, send_b)
@@ -387,24 +397,56 @@
 
     lax.fori_loop(0, chunks, drain, 0)
     for i in range(3):
-        share(i).wait()
-
-
-def finish(factor, out_hbm, gt_hbm, sums_ref, out_to, gt_to, ru_ref, lu_ref, ld_ref, rd_ref, sem):
-    copies = [pltpu.make_async_copy(out_hbm, out_to, sem.at[0]), pltpu.make_async_copy(gt_hbm, gt_to, sem.at[1])]
-    for copy in copies:
+        save(i).wait()
+
+
+def finish(
+    factor, out_hbm, gt_hbm, sums_hbm, out_to, gt_to, ru_to, lu_to, ld_to, rd_to,
+    held, sums_ref, ru_ref, lu_ref, ld_ref, rd_ref, sem, sum_sem, turn_sem,
+):
+    slabs = held.shape[1]
+    deep = out_hbm.shape[0] // slabs
+    enter, leave = [], []
+    sums = [pltpu.make_async_copy(sums_hbm.at[i], sums_ref.at[i], sum_sem.at[i]) for i in range(3)]
+    for p in range(slabs):
+        at = pl.ds(p * deep, deep)
+        for i, (source, target) in enumerate(((out_hbm, out_to), (gt_hbm, gt_to))):
+            enter.append(pltpu.make_async_copy(source.at[at], held.at[i, p], sem.at[0, i, p]))
+            leave.append(pltpu.make_async_copy(held.at[i, p], target.at[at], sem.at[1, i, p]))
+    for copy in enter[:2] + sums + enter[2:]:
         copy.start()
+    turned = [
+        pltpu.make_async_copy(source, target, turn_sem.at[i])
+        for i, (source, target) in enumerate(((ld_ref, ld_to), (lu_ref, lu_to), (rd_ref, rd_to), (ru_ref, ru_to)))
+    ]
+
+    def forward(part):
+        for i in part:
+            enter[i].wait()
+            leave[i].start()
+
     units = ld_ref.shape[1]
     size = sums_ref.shape[1] // 2
+    forward(range(0, 2))
+    sums[0].wait()
     for c in range(ld_ref.shape[0]):
         both = sums_ref[0, c * units:(c + 1) * units, :] * factor
         ld_ref[c] = both[:, :units]
         lu_ref[c] = both.T[units:, :]
+    turned[0].start()
+    turned[1].start()
+    forward(range(2, 4))
+    sums[1].wait()
     for s in range(2):
-        part = slice(s * size, (s + 1) * size)
-        rd_ref[s] = (sums_ref[1, part, :] * factor).T
-        ru_ref[s] = sums_ref[2, part, :] * factor
-    for copy in copies:
+        rd_ref[s] = (sums_ref[1, s * size:(s + 1) * size, :] * factor).T
+    turned[2].start()
+    forward(range(4, 6))
+    sums[2].wait()
+    for s in range(2):
+        ru_ref[s] = sums_ref[2, s * size:(s + 1) * size, :] * factor
+    turned[3].start()
+    forward(range(6, 2 * slabs))
+    for copy in leave + turned:
         copy.wait()
 
 
@@ -434,7 +476,7 @@
             jax.ShapeDtypeStruct((3, wide, 128), jnp.float32),
         ),
         in_specs=[hbm, hbm, vmem, vmem, hbm, hbm],
-        out_specs=(hbm, hbm, vmem),
+        out_specs=(hbm, hbm, hbm),
         scratch_shapes=[
             pltpu.VMEM((deep, count), bf), pltpu.VMEM((deep, count), bf),
             pltpu.VMEM(left_up.shape, bf), pltpu.VMEM(left_down.shape, bf),
@@ -455,12 +497,14 @@
             pltpu.VMEM((3, wide // 2, 128), jnp.float32),
             pltpu.VMEM((3, wide // 2, 128), bf),
             pltpu.VMEM((3, wide // 2, 128), bf),
+            pltpu.VMEM((3, wide, 128), jnp.float32),
             pltpu.SemaphoreType.DMA((4, chunks)),
             pltpu.SemaphoreType.DMA((4, chunks)),
             pltpu.SemaphoreType.DMA((3, 3)),
             pltpu.SemaphoreType.DMA((3, 3)),
             pltpu.SemaphoreType.DMA((6,)),
             pltpu.SemaphoreType.DMA((2, chunks)),
+            pltpu.SemaphoreType.DMA((3,)),
         ],
         compiler_params=pltpu.CompilerParams(
             collective_id=0, has_side_effects=True, vmem_limit_bytes=60 << 20
@@ -481,10 +525,16 @@
             jax.ShapeDtypeStruct(left_down.shape, jnp.float32),
             jax.ShapeDtypeStruct(right_down.shape, jnp.float32),
         ),
-        in_specs=[hbm, hbm, vmem],
-        out_specs=(hbm, hbm, vmem, vmem, vmem, vmem),
-        scratch_shapes=[pltpu.SemaphoreType.DMA((2,))],
-        compiler_params=pltpu.CompilerParams(vmem_limit_bytes=16 << 20),
+        in_specs=[hbm, hbm, hbm],
+        out_specs=(hbm,) * 6,
+        scratch_shapes=[
+            pltpu.VMEM((2, 4, deep // 4, count), bf),
+            pltpu.VMEM((3, wide, 128), jnp.float32),
+            pltpu.VMEM(right_up.shape, jnp.float32), pltpu.VMEM(left_up.shape, jnp.float32),
+            pltpu.VMEM(left_down.shape, jnp.float32), pltpu.VMEM(right_down.shape, jnp.float32),
+            pltpu.SemaphoreType.DMA((2, 2, 4)), pltpu.SemaphoreType.DMA((3,)), pltpu.SemaphoreType.DMA((4,)),
+        ],
+        compiler_params=pltpu.CompilerParams(vmem_limit_bytes=60 << 20),
         name="finish",
     )(output, grad_tokens, sums)
     return (output.reshape(shape), grad_tokens.reshape(shape), grad_ru, grad_lu, grad_ld, grad_rd)

time: 258 us -> 254 us (0.984)
  local copies, waits for them, and re-layouts: 4.03 us -> 0 us
    unnamed x6 -> x0, local copies, waits for them, and re-layouts: 4.03 us -> none
where the time goes in v3:
time: 254 us
  Pallas kernels  253 us (100%)
    pallas_call x1, Pallas kernels, shards(): pl.pallas_call(functools.partial(kernel, chunks, owners), out_shape=(jax....  250 us

profile of v3, /device:TPU:1, one launch (start us, length us, event | category | flops | bytes accessed | tf_op | source)
XLA Modules:
  0.0 254.1 jit_solution(16474398055429180646)
XLA Ops:
  0.6 249.6 %monarch.1 = (bf16[256,2560]{1,0:T(8,128)(2,1)}, bf16[256,2560]{1,0:T(8,128)(2,1)}, f32[3,1024,128]{2,1,0:T(8,128)}) custom-call(bf16[256,2560]{1,0:T(8,128)(2,1)} %bitcast.4, bf16[256,2560]{1,0:T(8,128)(2,1)} %bitcast.5, bf16[2,512,128]{2,1,0:T(8,128)(2,1)} %ru_ref.1, bf16[2,128,512]{2,1,0:T(8,128)(2,1)} %rd_ref.1, bf16[16,64,64]{2,1,0:T(8,128)(2,1)} %lu_hbm.1, ...), custom_call_target="tpu_custom_call" | custom-call | tf_op jit(solution)/shard_map/monarch/pallas_call | solution.py:471
  250.2 3.9 %finish.1 = (bf16[256,2560]{1,0:T(8,128)(2,1)}, bf16[256,2560]{1,0:T(8,128)(2,1)}, f32[2,512,128]{2,1,0:T(8,128)}, f32[16,64,64]{2,1,0:T(8,128)}, f32[16,64,64]{2,1,0:T(8,128)}, /*index=5*/f32[2,128,512]{2,1,0:T(8,128)}) custom-call(bf16[256,2560]{1,0:T(8,128)(2,1)} %get-tuple-element.15.out_hbm, bf16[256,2560]{1,0:T(8,128)(2,1)} %get-tuple-element.16.gt_hbm, ...), custom_call_target="tpu_custom_call" | custom-call | tf_op jit(solution)/shard_map/finish/pallas_call | solution.py:518

commit v4 on v3

--- a/solution.py
+++ b/solution.py
@@ -322,17 +322,13 @@
 
     def share(i):
         return pltpu.make_async_remote_copy(
-            src_ref=sums_ref.at[i, mine], dst_ref=sums_ref.at[i, mine],
+            src_ref=sums_ref.at[i], dst_ref=sums_hbm.at[i, mine],
             send_sem=sum_send.at[2, i], recv_sem=sum_recv.at[2, i],
             device_id=(core_peer, me), device_id_type=MESH,
         )
 
     def save(i):
-        return pltpu.make_async_copy(sums_ref.at[i], sums_hbm.at[i], save_sem.at[i])
-
-    def settle(i):
-        share(i).wait()
-        save(i).start()
+        return pltpu.make_async_copy(sums_ref.at[i], sums_hbm.at[i, mine], save_sem.at[i])
 
     def begin(i):
         pair(i).start()
@@ -344,8 +340,9 @@
 
     def finish(i):
         across(i).wait()
-        sums_ref[i, mine, :] = own[i].astype(jnp.float32) + far[i].astype(jnp.float32)
+        sums_ref[i] = own[i].astype(jnp.float32) + far[i].astype(jnp.float32)
         share(i).start()
+        save(i).start()
 
     lane = lax.broadcasted_iota(jnp.int32, (owners, 128), 1)
     for h in range(2):
@@ -383,11 +380,8 @@
     middle(2)
     finish(0)
     finish(1)
-    settle(0)
-    settle(1)
     finish(2)
 
-    settle(2)
     def drain(k, carry):
         sent(2, k, send_a)
         sent(3, k, send_b)
@@ -397,6 +391,7 @@
 
     lax.fori_loop(0, chunks, drain, 0)
     for i in range(3):
+        share(i).wait()
         save(i).wait()
 
 
@@ -497,7 +492,7 @@
             pltpu.VMEM((3, wide // 2, 128), jnp.float32),
             pltpu.VMEM((3, wide // 2, 128), bf),
             pltpu.VMEM((3, wide // 2, 128), bf),
-            pltpu.VMEM((3, wide, 128), jnp.float32),
+            pltpu.VMEM((3, wide // 2, 128), jnp.float32),
             pltpu.SemaphoreType.DMA((4, chunks)),
             pltpu.SemaphoreType.DMA((4, chunks)),
             pltpu.SemaphoreType.DMA((3, 3)),

time: 254 us -> 254 us (level)
  no operation moved by 1% of the time
where the time goes in v4:
time: 254 us; the launch traced here: 253 us
  Pallas kernels  253 us (100%)
    pallas_call x1, Pallas kernels, shards(): pl.pallas_call(functools.partial(kernel, chunks, owners), out_shape=(jax....  249 us

profile of v4, /device:TPU:1, one launch (start us, length us, event | category | flops | bytes accessed | tf_op | source)
XLA Modules:
  0.0 253.4 jit_solution(7412286861765101177)
XLA Ops:
  0.6 248.9 %monarch.1 = (bf16[256,2560]{1,0:T(8,128)(2,1)}, bf16[256,2560]{1,0:T(8,128)(2,1)}, f32[3,1024,128]{2,1,0:T(8,128)}) custom-call(bf16[256,2560]{1,0:T(8,128)(2,1)} %bitcast.4, bf16[256,2560]{1,0:T(8,128)(2,1)} %bitcast.5, bf16[2,512,128]{2,1,0:T(8,128)(2,1)} %ru_ref.1, bf16[2,128,512]{2,1,0:T(8,128)(2,1)} %rd_ref.1, bf16[16,64,64]{2,1,0:T(8,128)(2,1)} %lu_hbm.1, ...), custom_call_target="tpu_custom_call" | custom-call | tf_op jit(solution)/shard_map/monarch/pallas_call | solution.py:466
  249.5 3.9 %finish.1 = (bf16[256,2560]{1,0:T(8,128)(2,1)}, bf16[256,2560]{1,0:T(8,128)(2,1)}, f32[2,512,128]{2,1,0:T(8,128)}, f32[16,64,64]{2,1,0:T(8,128)}, f32[16,64,64]{2,1,0:T(8,128)}, /*index=5*/f32[2,128,512]{2,1,0:T(8,128)}) custom-call(bf16[256,2560]{1,0:T(8,128)(2,1)} %get-tuple-element.15.out_hbm, bf16[256,2560]{1,0:T(8,128)(2,1)} %get-tuple-element.16.gt_hbm, ...), custom_call_target="tpu_custom_call" | custom-call | tf_op jit(solution)/shard_map/finish/pallas_call | solution.py:513

commit v5 on v4

--- a/solution.py
+++ b/solution.py
@@ -8,9 +8,9 @@
 from jax.sharding import PartitionSpec as P
 
 MESH = pl.DeviceIdType.MESH
-CHUNK = 256
-AHEAD = 4
-LAG = 2
+CHUNK = 512
+AHEAD = 2
+LAG = 1
 SPAN = 256
 ROOT = 0.7978845608028654
 CUBIC = 0.044715

time: 254 us -> 253 us (level)
  no operation moved by 1% of the time
where the time goes in v5:
time: 253 us
  Pallas kernels  252 us (100%)
    pallas_call x1, Pallas kernels, shards(): pl.pallas_call(functools.partial(kernel, chunks, owners), out_shape=(jax....  249 us

profile of v5, /device:TPU:1, one launch (start us, length us, event | category | flops | bytes accessed | tf_op | source)
XLA Modules:
  0.0 253.0 jit_solution(11718480456929076582)
XLA Ops:
  0.6 248.5 %monarch.1 = (bf16[256,2560]{1,0:T(8,128)(2,1)}, bf16[256,2560]{1,0:T(8,128)(2,1)}, f32[3,1024,128]{2,1,0:T(8,128)}) custom-call(bf16[256,2560]{1,0:T(8,128)(2,1)} %bitcast.4, bf16[256,2560]{1,0:T(8,128)(2,1)} %bitcast.5, bf16[2,512,128]{2,1,0:T(8,128)(2,1)} %ru_ref.1, bf16[2,128,512]{2,1,0:T(8,128)(2,1)} %rd_ref.1, bf16[16,64,64]{2,1,0:T(8,128)(2,1)} %lu_hbm.1, ...), custom_call_target="tpu_custom_call" | custom-call | tf_op jit(solution)/shard_map/monarch/pallas_call | solution.py:466
  249.2 3.9 %finish.1 = (bf16[256,2560]{1,0:T(8,128)(2,1)}, bf16[256,2560]{1,0:T(8,128)(2,1)}, f32[2,512,128]{2,1,0:T(8,128)}, f32[16,64,64]{2,1,0:T(8,128)}, f32[16,64,64]{2,1,0:T(8,128)}, /*index=5*/f32[2,128,512]{2,1,0:T(8,128)}) custom-call(bf16[256,2560]{1,0:T(8,128)(2,1)} %get-tuple-element.15.out_hbm, bf16[256,2560]{1,0:T(8,128)(2,1)} %get-tuple-element.16.gt_hbm, ...), custom_call_target="tpu_custom_call" | custom-call | tf_op jit(solution)/shard_map/finish/pallas_call | solution.py:513
